TPU v7x, 256 devices: a whole 4x4x8 slice. The times are simulated.
256 devices in a mesh: pix: 16 (over y, x_hi, core), tm: 16 (over x_lo, z).
Axes of the slice: x: 4 (x_hi: 2, x_lo: 2; x = x_hi * 2 + x_lo), y: 4, z: 8, core: 2. Of those that a mesh axis runs over, the one named last changes fastest.
Arguments:
- raw_movie: float32 [128, 256, 8192], P('pix', None, 'tm'), may hold values from 0.05 to 2
- footprints: float32 [256, 32768], P('tm', 'pix'), may hold values from 0.05 to 1
- traces: float32 [256, 8192], P('pix', 'tm'), may hold values from 0.05 to 1
Outputs:
- denoised: float32 [128, 256, 8192], P('pix', None, 'tm')
- new_footprints: float32 [256, 32768], P('tm', 'pix')
- new_traces: float32 [256, 8192], P('pix', 'tm')
All inputs are finite; a program needn't handle non-finite values.
Results may differ from a plain program's by a relative error of at most 0.00013.
Values sent between devices are 32-bit elements; how exact they have to be, the bound alone decides.
A program may use at most 64 MiB of HBM per device.

v0:
```python
import jax
import jax.numpy as jnp
from jax import lax
from jax.sharding import PartitionSpec as P

edge_scale = 0.5
step_size = 0.24


def with_halo(cells, sides, width):
    for axis, dim in sides:
        count = lax.axis_size(axis)
        ends = count - 1
        head = lax.slice_in_dim(cells, 0, width, axis=dim)
        tail = lax.slice_in_dim(cells, cells.shape[dim] - width, cells.shape[dim], axis=dim)
        cells = jnp.concatenate(
            [
                lax.ppermute(tail, axis, [(i, (i + 1) % count) for i in range(ends)]),
                cells,
                lax.ppermute(head, axis, [((i + 1) % count, i) for i in range(ends)]),
            ],
            axis=dim,
        )
    return cells


def flux_term(change):
    return change / (1.0 + change / edge_scale * (change / edge_scale))


def substep(extended):
    middle = extended[1:-1]
    padded = jnp.pad(middle, ((0, 0), (1, 1), (0, 0)))
    summed = flux_term(extended[:-2] - middle) + flux_term(extended[2:] - middle)
    summed = summed + flux_term(padded[:, :-2] - middle) + flux_term(padded[:, 2:] - middle)
    return middle + step_size * summed


def matmul_hi(left, right):
    return jnp.dot(left, right, precision=lax.Precision.HIGHEST, preferred_element_type=jnp.float32)


def contract_last(left, right):
    return lax.dot_general(
        left,
        right,
        (((1,), (1,)), ((), ())),
        precision=lax.Precision.HIGHEST,
        preferred_element_type=jnp.float32,
    )


def body(raw_movie, footprints, traces):
    row_count = raw_movie.shape[0]
    col_count = raw_movie.shape[1]
    frame_count = raw_movie.shape[2]
    current = raw_movie
    for repeat in range(4):
        extended = with_halo(current, (("pix", 0),), 1)
        current = substep(extended)
    pixels = current.reshape(row_count * col_count, frame_count)
    foot_full = lax.all_gather(footprints, "tm", axis=0, tiled=True)
    trace_full = lax.all_gather(traces, "pix", axis=0, tiled=True)
    rank_block = traces.shape[0]
    rank_start = lax.axis_index("pix") * rank_block
    part = foot_full
    numerator = lax.psum_scatter(matmul_hi(part, pixels), "pix", scatter_dimension=0, tiled=True)
    gram = lax.psum(contract_last(foot_full, foot_full), "pix")
    gram_rows = lax.dynamic_slice_in_dim(gram, rank_start, rank_block, 0)
    new_traces = traces * numerator / matmul_hi(gram_rows, trace_full)
    new_full = lax.all_gather(new_traces, "pix", axis=0, tiled=True)
    foot_block = footprints.shape[0]
    foot_start = lax.axis_index("tm") * foot_block
    part = new_full
    foot_numerator = lax.psum_scatter(
        contract_last(part, pixels), "tm", scatter_dimension=0, tiled=True
    )
    trace_gram = lax.psum(contract_last(new_full, new_full), "tm")
    trace_rows = lax.dynamic_slice_in_dim(trace_gram, foot_start, foot_block, 0)
    new_footprints = footprints * foot_numerator / matmul_hi(trace_rows, foot_full)
    return (current, new_footprints, new_traces)


def solution(mesh):
    placed = (P("pix", None, "tm"), P("tm", "pix"), P("pix", "tm"))
    return jax.shard_map(
        body,
        mesh=mesh,
        in_specs=placed,
        out_specs=(P("pix", None, "tm"), P("tm", "pix"), P("pix", "tm")),
        check_vma=False,
    )
```

profile of v0, /device:TPU:2, one launch (start us, length us, event | category | flops | bytes accessed | tf_op | source)
XLA Modules:
  0.0 602.0 jit_solution(13072026490475913355)
XLA Ops:
  8.5 1.8 collective-permute-start
  11.8 4.2 collective-permute-done.1
  15.9 9.9 %multiply_add_fusion.3 = f32[8,256,512]{2,1,0:T(8,128)S(1)} fusion(f32[8,256,512]{2,1,0:T(8,128)} %param.3, f32[1,256,512]{2,1,0:T(8,128)S(1)} %collective-permute-done.1, f32[1,256,512]{2,1,0:T(8,128)S(1)} %collective-permute-done), kind=kLoop, calls=%fused_computation.19 | loop fusion | flops 28311552 | bytes 9437184 | tf_op jit(solution)/shard_map/add | solution.py:36
  25.9 12.9 %collective-permute-start.2 = (f32[1,256,512]{2,1,0:T(8,128)S(1)}, f32[1,256,512]{2,1,0:T(8,128)S(1)}, u32[]{:S(2)}, u32[]{:S(2)}) collective-permute-start(f32[1,256,512]{2,1,0:T(8,128)S(1)} %get-tuple-element.10), channel_id=1, source_target_pairs={{0,16},{16,32},{32,48},{48,64},{64,80},{80,96},{96,112},{112,128},... | collective-permute-start | bytes 1572872 | tf_op jit(solution)/shard_map/ppermute | solution.py:18
  40.4 2.3 collective-permute-done.3
  42.7 4.5 multiply_add_fusion.2
  47.2 2.0 copy-done.1
  49.3 12.1 %collective-permute-start.4 = (f32[1,256,512]{2,1,0:T(8,128)S(1)}, f32[1,256,512]{2,1,0:T(8,128)S(1)}, u32[]{:S(2)}, u32[]{:S(2)}) collective-permute-start(f32[1,256,512]{2,1,0:T(8,128)S(1)} %get-tuple-element.8), channel_id=1, source_target_pairs={{0,16},{16,32},{32,48},{48,64},{64,80},{80,96},{96,112},{112,128},... | collective-permute-start | bytes 1572872 | tf_op jit(solution)/shard_map/ppermute | solution.py:18
  62.9 2.3 collective-permute-done.5
  65.3 9.9 %multiply_add_fusion.1 = f32[8,256,512]{2,1,0:T(8,128)S(1)} fusion(f32[8,256,512]{2,1,0:T(8,128)} %copy-done.1, f32[1,256,512]{2,1,0:T(8,128)S(1)} %collective-permute-done.5, f32[1,256,512]{2,1,0:T(8,128)S(1)} %collective-permute-done.4), kind=kLoop, calls=%fused_computation.17 | loop fusion | flops 28311552 | bytes 9437184 | tf_op jit(solution)/shard_map/add | solution.py:36
  75.2 12.4 %collective-permute-start.6 = (f32[1,256,512]{2,1,0:T(8,128)S(1)}, f32[1,256,512]{2,1,0:T(8,128)S(1)}, u32[]{:S(2)}, u32[]{:S(2)}) collective-permute-start(f32[1,256,512]{2,1,0:T(8,128)S(1)} %get-tuple-element.6), channel_id=1, source_target_pairs={{0,16},{16,32},{32,48},{48,64},{64,80},{80,96},{96,112},{112,128},... | collective-permute-start | bytes 1572872 | tf_op jit(solution)/shard_map/ppermute | solution.py:18
  89.1 2.3 collective-permute-done.7
  91.4 5.5 multiply_add_fusion
  96.9 41.0 %all-gather.2.cloned.1.call-done = f32[256,2048]{1,0:T(8,128)} async-done(((f32[16,2048]{1,0:T(8,128)}), f32[256,2048]{1,0:T(8,128)}) %all-gather.2.cloned.1.call-update) | async-done | bytes 2097168 | tf_op jit(solution)/shard_map/all_gather | solution.py:62
  137.9 4.9 fusion.17
  143.1 8.6 %convolution_bitcast_fusion = f32[256,512]{0,1:T(8,128)S(1)} fusion(f32[2048,512]{1,0:T(8,128)} %bitcast.14, f32[256,2048]{1,0:T(8,128)S(1)} %copy-done), kind=kOutput, calls=%fused_computation.20 | convolution fusion | flops 3221225472 | bytes 6815744 | tf_op jit(solution)/shard_map/dot_general | solution.py:40
  152.8 26.6 %all_gather.10 = f32[256,512]{1,0:T(8,128)S(1)} all-gather(f32[16,512]{1,0:T(8,128)S(1)} %copy-done.3), channel_id=1, replica_groups=mesh['pix'=16,'tm'=16] {'pix'}, dimensions={0}, use_global_device_ids=true | all-gather | bytes 557056 | tf_op jit(solution)/shard_map/all_gather | solution.py:63
  179.3 104.3 %all-reduce.7.cloned.1.call-done = f32[256,256]{1,0:T(8,128)} async-done(((f32[256,256]{1,0:T(8,128)}), f32[256,256]{1,0:T(8,128)}) %all-reduce.7.cloned.1.call-update) | async-done | bytes 262160 | tf_op jit(solution)/shard_map/psum | solution.py:68
  283.6 78.4 %reduce-scatter.7.cloned.1.call-done = f32[16,512]{1,0:T(8,128)} async-done(((f32[256,512]{1,0:T(8,128)}), f32[16,512]{1,0:T(8,128)}) %reduce-scatter.7.cloned.1.call-update) | async-done | bytes 32784 | tf_op jit(solution)/shard_map/reduce_scatter | solution.py:67
  363.2 24.3 %all_gather.11 = f32[256,512]{1,0:T(8,128)S(1)} all-gather(f32[16,512]{1,0:T(8,128)S(1)} %convolution_divide_fusion), channel_id=1, replica_groups=mesh['pix'=16,'tm'=16] {'pix'}, dimensions={0}, use_global_device_ids=true | all-gather | bytes 557056 | tf_op jit(solution)/shard_map/all_gather | solution.py:71
  388.9 7.2 %fusion.18 = f32[256,2048]{1,0:T(8,128)} fusion(f32[256,512]{1,0:T(8,128)S(1)} %all_gather.11, f32[2048,512]{1,0:T(8,128)} %bitcast.15), kind=kOutput, calls=%fused_computation.33 | convolution fusion | flops 3221225472 | bytes 6815744 | tf_op jit(solution)/shard_map/dot_general | solution.py:44
  396.1 123.7 %all-reduce.9.cloned.1.call-done = f32[256,256]{1,0:T(8,128)} async-done(((f32[256,256]{1,0:T(8,128)}), f32[256,256]{1,0:T(8,128)}) %all-reduce.9.cloned.1.call-update) | async-done | bytes 262160 | tf_op jit(solution)/shard_map/psum | solution.py:78
  519.9 1.8 fusion.8
  521.7 72.2 %reduce-scatter.5.cloned.1.call-done = f32[16,2048]{1,0:T(8,128)} async-done(((f32[256,2048]{1,0:T(8,128)}), f32[16,2048]{1,0:T(8,128)}) %reduce-scatter.5.cloned.1.call-update) | async-done | bytes 131088 | tf_op jit(solution)/shard_map/reduce_scatter | solution.py:75
  (35 shorter events, 12.9 us)
Async XLA Ops:
  7.2 130.7 %all-gather.2.cloned.1.call-start = ((), (), s32[]{:S(2)}) async-start(), calls=%async_computation.2 | async-start | bytes 2228224 | tf_op jit(solution)/shard_map/all_gather | solution.py:62
  8.5 3.3 collective-permute-start
  10.3 5.7 collective-permute-start.1
  25.9 14.4 %collective-permute-start.2 = (f32[1,256,512]{2,1,0:T(8,128)S(1)}, f32[1,256,512]{2,1,0:T(8,128)S(1)}, u32[]{:S(2)}, u32[]{:S(2)}) collective-permute-start(f32[1,256,512]{2,1,0:T(8,128)S(1)} %get-tuple-element.10), channel_id=1, source_target_pairs={{0,16},{16,32},{32,48},{48,64},{64,80},{80,96},{96,112},{112,128},... | collective-permute-start | bytes 1572872 | tf_op jit(solution)/shard_map/ppermute | solution.py:18
  38.9 3.8 collective-permute-start.3
  47.2 2.0 copy-start.1
  49.3 13.6 %collective-permute-start.4 = (f32[1,256,512]{2,1,0:T(8,128)S(1)}, f32[1,256,512]{2,1,0:T(8,128)S(1)}, u32[]{:S(2)}, u32[]{:S(2)}) collective-permute-start(f32[1,256,512]{2,1,0:T(8,128)S(1)} %get-tuple-element.8), channel_id=1, source_target_pairs={{0,16},{16,32},{32,48},{48,64},{64,80},{80,96},{96,112},{112,128},... | collective-permute-start | bytes 1572872 | tf_op jit(solution)/shard_map/ppermute | solution.py:18
  61.4 3.8 collective-permute-start.5
  62.8 220.9 %all-reduce.7.cloned.1.call-start = ((), (), s32[]{:S(2)}) async-start(), calls=%async_computation.3 | async-start | bytes 524288 | tf_op jit(solution)/shard_map/psum | solution.py:68
  75.2 13.9 %collective-permute-start.6 = (f32[1,256,512]{2,1,0:T(8,128)S(1)}, f32[1,256,512]{2,1,0:T(8,128)S(1)}, u32[]{:S(2)}, u32[]{:S(2)}) collective-permute-start(f32[1,256,512]{2,1,0:T(8,128)S(1)} %get-tuple-element.6), channel_id=1, source_target_pairs={{0,16},{16,32},{32,48},{48,64},{64,80},{80,96},{96,112},{112,128},... | collective-permute-start | bytes 1572872 | tf_op jit(solution)/shard_map/ppermute | solution.py:18
  87.6 3.8 collective-permute-start.7
  137.9 5.2 copy-start
  142.9 219.2 %reduce-scatter.7.cloned.1.call-start = ((), (), s32[]{:S(2)}) async-start(), calls=%async_computation.6 | async-start | bytes 557056 | tf_op jit(solution)/shard_map/reduce_scatter | solution.py:67
  143.1 9.7 %copy-start.3 = (f32[16,512]{1,0:T(8,128)S(1)}, f32[16,512]{1,0:T(8,128)}, u32[]{:S(2)}) copy-start(f32[16,512]{1,0:T(8,128)} %param.5) | copy-start | bytes 98308
  152.7 367.2 %all-reduce.9.cloned.1.call-start = ((), (), s32[]{:S(2)}) async-start(), calls=%async_computation.5 | async-start | bytes 524288 | tf_op jit(solution)/shard_map/psum | solution.py:78
  363.2 32.9 %copy-start.4 = (f32[16,512]{1,0:T(8,128)}, f32[16,512]{1,0:T(8,128)S(1)}, u32[]{:S(2)}) copy-start(f32[16,512]{1,0:T(8,128)S(1)} %convolution_divide_fusion) | copy-start | bytes 98308
  388.9 205.0 %copy-start.2 = (f32[16,2048]{1,0:T(8,128)S(1)}, f32[16,2048]{1,0:T(8,128)}, u32[]{:S(2)}) copy-start(f32[16,2048]{1,0:T(8,128)} %param.4) | copy-start | bytes 393220
  388.9 205.0 %reduce-scatter.5.cloned.1.call-start = ((), (), s32[]{:S(2)}) async-start(), calls=%async_computation.4 | async-start | bytes 2228224 | tf_op jit(solution)/shard_map/reduce_scatter | solution.py:75
Sparse Core Ops, SparseCore 0:
  62.9 74.9 all-gather.1
  143.0 140.6 all-reduce.6
  288.2 73.8 reduce-scatter.6
  389.0 130.8 all-reduce.8
  522.4 71.4 reduce-scatter.4
where the time goes:
time: 604 us; the launch traced here: 602 us
  waiting for transfers between devices  432 us (72%)
  blocking collectives  50.9 us (8%)
  starting transfers between devices  44.8 us (7%)
  other arithmetic  31.4 us (5%)
  matrix products  24.9 us (4%)
  between operations  14 us (2%)
    psum x1, waiting for transfers between devices, body(): trace_gram = lax.psum(contract_last(new_full, new_full), 'tm')  124 us
    psum x1, waiting for transfers between devices, body(): gram = lax.psum(contract_last(foot_full, foot_full), 'pix')  104 us
    reduce_scatter x1, waiting for transfers between devices, body(): lax.psum_scatter(matmul_hi(part, pixels), 'pix', scatter_dimension=0, til...  78.4 us
    reduce_scatter x1, waiting for transfers between devices, body(): lax.psum_scatter(contract_last(part, pixels), 'tm', scatter_dimension=0,...  72.2 us
    all_gather x1, waiting for transfers between devices, body(): foot_full = lax.all_gather(footprints, 'tm', axis=0, tiled=True)  41 us
    ppermute x4, starting transfers between devices, with_halo(): lax.ppermute(tail, axis, [(i, (i + 1) % count) for i in range(ends)])  39.2 us
    add x4, other arithmetic, substep(): return middle + step_size * summed  29.8 us
    all_gather x1, blocking collectives, body(): trace_full = lax.all_gather(traces, 'pix', axis=0, tiled=True)  26.6 us
  transfers between devices with their start and end apart: 13, of which 13 were waited for; matrix products, arithmetic and copies ran while one was open for 6% of the time, Pallas kernels for 0%

commit v1 on v0

v1 whole, which is shorter than its diff:
```python
import jax
import jax.numpy as jnp
from jax import lax
from jax.experimental import pallas as pl
from jax.experimental.pallas import tpu as pltpu
from jax.sharding import PartitionSpec as P

F32 = jnp.float32
BF16 = jnp.bfloat16
MESH = pl.DeviceIdType.MESH
HALO = 4
ROWS = 8
EXT = ROWS + 2 * HALO
COLS = 256
FRAMES = 512
CHUNK = 128
CHUNKS = FRAMES // CHUNK
RANK = 256
BLK = 16
NB = RANK // BLK
CHIPS = 8
NPIX = 16
NZ = 8
LOCAL = ROWS * COLS
WIDE = LOCAL + RANK
STEP = 0.24


def split(x):
    hi = x.astype(BF16)
    return hi, (x - hi.astype(F32)).astype(BF16)


def dot3(ah, al, bh, bl, rhs_dim):
    dims = (((1,), (rhs_dim,)), ((), ()))

    def one(a, b):
        return lax.dot_general(a, b, dims, preferred_element_type=F32)

    return one(ah, bh) + (one(al, bh) + one(ah, bl))


def flux_den(c):
    return 1.0 + 4.0 * (c * c)


def kernel(
    raw, foot, traces, den_out, foot_out, trace_out,
    y_buf, fd_buf, ph, plo, ff, fh8, fl8, fn, lu, ld, lx, gp, gcr, gl, tf, scale_buf,
    np_buf, cr_buf, lc_buf, nf,
    loc_sem, out_sem, halo_s, halo_r, fx_s, fx_r, fr_s, fr_r, ring_s, ring_r, rx_s, rx_r,
    core_s, core_r, chip_s, chip_r,
):
    p = lax.axis_index("pix")
    t = lax.axis_index("tm")
    chip = p // 2
    core = p % 2
    xl = t // NZ
    z = t % NZ
    up = (p, xl * NZ + (z + 1) % NZ)
    down = (p, xl * NZ + (z + NZ - 1) % NZ)
    across = (p, (1 - xl) * NZ + z)
    sibling = (chip * 2 + (1 - core), t)
    pending = []

    def remote(src, dst, ssem, rsem, dev):
        return pltpu.make_async_remote_copy(
            src_ref=src, dst_ref=dst, send_sem=ssem, recv_sem=rsem, device_id=dev, device_id_type=MESH
        )

    def send(*args):
        cp = remote(*args)
        cp.start()
        pending.append(cp)
        return cp

    def peer_chip(i):
        return ((lax.rem(chip + i, CHIPS)) * 2 + core, t)

    loads = []
    for c in range(CHUNKS):
        cp = pltpu.make_async_copy(
            raw.at[:, :, pl.ds(c * CHUNK, CHUNK)], y_buf.at[c, pl.ds(HALO, ROWS)], loc_sem.at[c]
        )
        cp.start()
        loads.append(cp)
    foot_load = pltpu.make_async_copy(foot, ff.at[t], loc_sem.at[CHUNKS])
    foot_load.start()
    trace_load = pltpu.make_async_copy(traces, tf.at[chip, core], loc_sem.at[CHUNKS + 1])
    trace_load.start()

    halo_far = (lax.rem(p + NPIX + 2 * core - 1, NPIX), t)
    partners = [sibling, halo_far, across, up, down] + [peer_chip(i) for i in range(1, CHIPS)]
    bar = pltpu.get_barrier_semaphore()
    for dev in partners:
        pl.semaphore_signal(bar, inc=1, device_id=dev, device_id_type=MESH)

    @pl.when(p == 0)
    def _():
        for c in range(CHUNKS):
            y_buf[c, pl.ds(0, HALO)] = jnp.zeros((HALO, COLS, CHUNK), F32)

    @pl.when(p == NPIX - 1)
    def _():
        for c in range(CHUNKS):
            y_buf[c, pl.ds(HALO + ROWS, HALO)] = jnp.zeros((HALO, COLS, CHUNK), F32)

    pl.semaphore_wait(bar, len(partners))

    def halo_down(c):
        return remote(
            raw.at[pl.ds(ROWS - HALO, HALO), :, pl.ds(c * CHUNK, CHUNK)],
            y_buf.at[c, pl.ds(0, HALO)], halo_s.at[0, c], halo_r.at[0, c],
            (lax.rem(p + 1, NPIX), t),
        )

    def halo_up(c):
        return remote(
            raw.at[pl.ds(0, HALO), :, pl.ds(c * CHUNK, CHUNK)],
            y_buf.at[c, pl.ds(HALO + ROWS, HALO)], halo_s.at[1, c], halo_r.at[1, c],
            (lax.rem(p + NPIX - 1, NPIX), t),
        )

    def halo_start(c):
        @pl.when(p < NPIX - 1)
        def _():
            halo_down(c).start()

        @pl.when(p > 0)
        def _():
            halo_up(c).start()

    def halo_wait(c):
        @pl.when(p > 0)
        def _():
            halo_down(c).wait_recv()

        @pl.when(p < NPIX - 1)
        def _():
            halo_up(c).wait_recv()

    def halo_wait_send(c):
        @pl.when(p < NPIX - 1)
        def _():
            halo_down(c).wait_send()

        @pl.when(p > 0)
        def _():
            halo_up(c).wait_send()

    def fblock(j, dz):
        col = xl if j == 1 else 1 - xl
        return col * NZ + lax.rem(z + dz + 2 * NZ, NZ)

    def foot_send(s, j):
        cps = []
        for d in range(2):
            if s == 3 and d == j:
                continue
            sign = -1 if d == 0 else 1
            b = fblock(j, sign * s)
            src = foot if (s == 0 and j == 1) else ff.at[b]
            cps.append(send(src, ff.at[b], fr_s.at[d, s, j], fr_r.at[d, s, j], up if d == 0 else down))
        return cps

    def wait_all(cps):
        for cp in cps:
            cp.wait_recv()

    def gather_chips(src, dst, slot):
        cps = []
        for i in range(1, CHIPS):
            cps.append(send(src, dst, chip_s.at[slot, i], chip_r.at[slot, i], peer_chip(i)))
        return cps

    def diffuse(c):
        def substep(s, carry):
            src = jnp.where(lax.rem(s, 2) == 1, c, CHUNKS)
            dst = jnp.where(lax.rem(s, 2) == 1, CHUNKS, c)
            col = lax.broadcasted_iota(jnp.int32, (COLS, CHUNK), 0)
            first = s - 1
            c0 = y_buf[src, first + 1] - y_buf[src, first]
            fd_buf[...] = c0 / flux_den(c0)

            def row(r, carry):
                u = y_buf[src, r]
                cd = y_buf[src, r + 1] - u
                ur = jnp.where(col == COLS - 1, 0.0, pltpu.roll(u, COLS - 1, 0))
                cr = ur - u
                dd = flux_den(cd)
                dr = flux_den(cr)
                inv = 1.0 / (dd * dr)
                fdn = cd * (dr * inv)
                frt = cr * (dd * inv)
                u0 = u[0:8]
                edge = u0 / flux_den(u0)
                edge = jnp.concatenate([edge, frt[8:]], axis=0)
                fl = jnp.where(col == 0, edge, pltpu.roll(frt, 1, 0))
                total = (fdn - fd_buf[...]) + (frt - fl)
                fd_buf[...] = fdn
                new = u + STEP * total
                outside = ((p == 0) & (r < HALO)) | ((p == NPIX - 1) & (r >= HALO + ROWS))
                y_buf[dst, r] = jnp.where(outside, 0.0, new)
                return carry

            return lax.fori_loop(s, EXT - s, row, carry)

        lax.fori_loop(1, HALO + 1, substep, 0)
        for r in range(ROWS):
            hi, lo = split(y_buf[c, HALO + r])
            ph[c, r] = hi
            plo[c, r] = lo

    def numerator(c):
        def body(r, acc):
            return acc + dot3(fh8[r], fl8[r], ph[c, r], plo[c, r], 0)

        part = lax.fori_loop(0, ROWS, body, jnp.zeros((RANK, CHUNK), F32))
        np_buf[c] = part.reshape(CHIPS, 2, BLK, CHUNK)

    def rs_core(c):
        return send(np_buf.at[c, :, 1 - core], cr_buf.at[c], core_s.at[c], core_r.at[c], sibling)

    def rs_chips(c, cp):
        cp.wait_recv()
        cr_buf[c] = cr_buf[c] + np_buf[c, :, core]
        cps = []
        for i in range(1, CHIPS):
            cps.append(
                send(
                    cr_buf.at[c, lax.rem(chip + i, CHIPS)], lc_buf.at[c, i],
                    chip_s.at[c, i], chip_r.at[c, i], peer_chip(i),
                )
            )
        return cps

    def ag_chips(c, cps):
        wait_all(cps)
        num = cr_buf[c, chip]
        for i in range(1, CHIPS):
            num = num + lc_buf[c, i]
        new = num * scale_buf[:, c * CHUNK : (c + 1) * CHUNK]
        trace_out[:, c * CHUNK : (c + 1) * CHUNK] = new
        nf[c, chip, core] = new
        return gather_chips(nf.at[c, chip, core], nf.at[c, chip, core], CHUNKS + c)

    def ag_core(c, cps):
        wait_all(cps)
        return send(
            nf.at[c, :, core], nf.at[c, :, core], core_s.at[CHUNKS + c], core_r.at[CHUNKS + c], sibling
        )

    def foot_update(c, cp):
        cp.wait_recv()
        nh, nl = split(nf[c].reshape(RANK, CHUNK))
        first = c == 0

        def put(where, val):
            val = val.reshape(NB, BLK, RANK)
            fn[:, :, where] = val if first else fn[:, :, where] + val

        put(pl.ds(LOCAL, RANK), dot3(nh, nl, nh, nl, 1))

        def body(r, carry):
            put(pl.ds(pl.multiple_of(r * COLS, COLS), COLS), dot3(nh, nl, ph[c, r], plo[c, r], 1))
            return carry

        lax.fori_loop(0, ROWS, body, 0)

    halo_start(0)
    fx = send(foot, ff.at[t], fx_s.at[0], fx_r.at[0], across)
    own0 = foot_send(0, 1)
    tr = gather_chips(traces, tf.at[chip, core], 2 * CHUNKS)
    halo_start(1)
    fx.wait_recv()
    oth0 = foot_send(0, 0)
    wait_all(own0)
    own1 = foot_send(1, 1)
    wait_all(oth0)
    oth1 = foot_send(1, 0)
    wait_all(tr)
    trace_load.wait()
    tr_core = send(tf.at[:, core], tf.at[:, core], core_s.at[2 * CHUNKS], core_r.at[2 * CHUNKS], sibling)
    wait_all(own1)
    own2 = foot_send(2, 1)
    wait_all(oth1)
    oth2 = foot_send(2, 0)
    for cp in loads:
        cp.wait()
    halo_wait(0)
    halo_start(2)
    diffuse(0)
    stores = []

    def store(c):
        cp = pltpu.make_async_copy(
            y_buf.at[c, pl.ds(HALO, ROWS)], den_out.at[:, :, pl.ds(c * CHUNK, CHUNK)], out_sem.at[c]
        )
        cp.start()
        stores.append(cp)

    store(0)
    wait_all(own2)
    own3 = foot_send(3, 1)
    wait_all(oth2)
    oth3 = foot_send(3, 0)
    foot_load.wait()
    halo_wait(1)
    halo_start(3)
    diffuse(1)
    store(1)
    wait_all(own3)
    wait_all(oth3)

    def split_foot(r, carry):
        hi, lo = split(ff[:, :, pl.ds(pl.multiple_of(r * COLS, COLS), COLS)].reshape(RANK, COLS))
        fh8[r] = hi
        fl8[r] = lo
        return carry

    lax.fori_loop(0, ROWS, split_foot, 0)

    def gram_body(r, acc):
        return acc + dot3(fh8[r], fl8[r], fh8[r], fl8[r], 1)

    gp[...] = lax.fori_loop(0, ROWS, gram_body, jnp.zeros((RANK, RANK), F32)).reshape(CHIPS, 2, BLK, RANK)
    gslot = 2 * CHUNKS + 1
    g_core = send(gp.at[:, 1 - core], gcr, core_s.at[gslot], core_r.at[gslot], sibling)
    numerator(0)
    rs0 = rs_core(0)
    g_core.wait_recv()
    gcr[...] = gcr[...] + gp[:, core]
    g_chips = []
    for i in range(1, CHIPS):
        g_chips.append(
            send(gcr.at[lax.rem(chip + i, CHIPS)], gl.at[i], chip_s.at[gslot, i], chip_r.at[gslot, i], peer_chip(i))
        )
    rs0 = rs_chips(0, rs0)
    numerator(1)
    rs1 = rs_core(1)
    rs1 = rs_chips(1, rs1)
    wait_all(g_chips)
    gram = gcr[chip]
    for i in range(1, CHIPS):
        gram = gram + gl[i]
    tr_core.wait_recv()
    gh, gl_ = split(gram)
    th, tl = split(tf[...].reshape(RANK, FRAMES))
    scale_buf[...] = tf[chip, core] / dot3(gh, gl_, th, tl, 0)
    ag0 = ag_chips(0, rs0)
    halo_wait(2)
    diffuse(2)
    store(2)
    ag0 = ag_core(0, ag0)
    ag1 = ag_chips(1, rs1)
    numerator(2)
    rs2 = rs_core(2)
    foot_update(0, ag0)
    rs2 = rs_chips(2, rs2)
    ag1 = ag_core(1, ag1)
    foot_update(1, ag1)
    halo_wait(3)
    diffuse(3)
    store(3)
    ag2 = ag_chips(2, rs2)
    numerator(3)
    rs3 = rs_core(3)
    rs3 = rs_chips(3, rs3)
    ag2 = ag_core(2, ag2)
    foot_update(2, ag2)
    ag3 = ag_chips(3, rs3)
    ag3 = ag_core(3, ag3)
    foot_update(3, ag3)

    def ring_send(s, j, got):
        cps = []
        for d in range(2):
            if s == 0 and d == j:
                continue
            land = lu if d == 0 else ld
            b = fblock(j, (NZ // 2 - s) * (1 if d == 0 else -1))
            if d in got:
                land[s - 1, j] = land[s - 1, j] + fn[b]
                src = land.at[s - 1, j]
            else:
                src = fn.at[b]
            cps.append(send(src, land.at[s, j], ring_s.at[d, s, j], ring_r.at[d, s, j], up if d == 0 else down))
        return cps

    r0 = ring_send(0, 0, ())
    r1 = ring_send(0, 1, ())
    for s in range(1, 4):
        wait_all(r0)
        r0 = ring_send(s, 0, (1,) if s == 1 else (0, 1))
        wait_all(r1)
        r1 = ring_send(s, 1, (0,) if s == 1 else (0, 1))
    wait_all(r0)
    bo = fblock(0, 0)
    lu[3, 0] = (lu[3, 0] + ld[3, 0]) + fn[bo]
    rx = send(lu.at[3, 0], lx, rx_s.at[0], rx_r.at[0], across)
    wait_all(r1)
    lu[3, 1] = (lu[3, 1] + ld[3, 1]) + fn[fblock(1, 0)]
    rx.wait_recv()
    kh, kl = split(lu[3, 1, :, pl.ds(LOCAL, RANK)] + lx[:, pl.ds(LOCAL, RANK)])

    def final(r, carry):
        w = pl.ds(pl.multiple_of(r * COLS, COLS), COLS)
        den = dot3(kh, kl, fh8[r], fl8[r], 0)
        foot_out[:, w] = ff[t, :, w] * (lu[3, 1, :, w] + lx[:, w]) / den
        return carry

    lax.fori_loop(0, ROWS, final, 0)

    for cp in pending:
        cp.wait_send()
    for c in range(CHUNKS):
        halo_wait_send(c)
    for cp in stores:
        cp.wait()


def body(raw_movie, footprints, traces):
    dma = pltpu.SemaphoreType.DMA
    vm = pltpu.VMEM
    hbm = pl.BlockSpec(memory_space=pltpu.MemorySpace.HBM)
    inv = pl.BlockSpec(memory_space=pltpu.MemorySpace.VMEM)
    return pl.pallas_call(
        kernel,
        out_shape=(
            jax.ShapeDtypeStruct(raw_movie.shape, F32),
            jax.ShapeDtypeStruct(footprints.shape, F32),
            jax.ShapeDtypeStruct(traces.shape, F32),
        ),
        in_specs=[hbm, hbm, hbm],
        out_specs=(hbm, inv, inv),
        scratch_shapes=[
            vm((CHUNKS + 1, EXT, COLS, CHUNK), F32),
            vm((COLS, CHUNK), F32),
            vm((CHUNKS, ROWS, COLS, CHUNK), BF16),
            vm((CHUNKS, ROWS, COLS, CHUNK), BF16),
            vm((NB, BLK, LOCAL), F32),
            vm((ROWS, RANK, COLS), BF16),
            vm((ROWS, RANK, COLS), BF16),
            vm((NB, BLK, WIDE), F32),
            vm((4, 2, BLK, WIDE), F32),
            vm((4, 2, BLK, WIDE), F32),
            vm((BLK, WIDE), F32),
            vm((CHIPS, 2, BLK, RANK), F32),
            vm((CHIPS, BLK, RANK), F32),
            vm((CHIPS, BLK, RANK), F32),
            vm((CHIPS, 2, BLK, FRAMES), F32),
            vm((BLK, FRAMES), F32),
            vm((CHUNKS, CHIPS, 2, BLK, CHUNK), F32),
            vm((CHUNKS, CHIPS, BLK, CHUNK), F32),
            vm((CHUNKS, CHIPS, BLK, CHUNK), F32),
            vm((CHUNKS, CHIPS, 2, BLK, CHUNK), F32),
            dma((CHUNKS + 2,)),
            dma((CHUNKS,)),
            dma((2, CHUNKS)),
            dma((2, CHUNKS)),
            dma((1,)),
            dma((1,)),
            dma((2, 4, 2)),
            dma((2, 4, 2)),
            dma((2, 4, 2)),
            dma((2, 4, 2)),
            dma((1,)),
            dma((1,)),
            dma((2 * CHUNKS + 2,)),
            dma((2 * CHUNKS + 2,)),
            dma((2 * CHUNKS + 2, CHIPS)),
            dma((2 * CHUNKS + 2, CHIPS)),
        ],
        compiler_params=pltpu.CompilerParams(
            collective_id=0, has_side_effects=True, vmem_limit_bytes=48 * 1024 * 1024
        ),
        cost_estimate=pl.CostEstimate(flops=4 * 10**9, bytes_accessed=16 * 2**20, transcendentals=0),
    )(raw_movie, footprints, traces)


def solution(mesh):
    placed = (P("pix", None, "tm"), P("tm", "pix"), P("pix", "tm"))
    return jax.shard_map(body, mesh=mesh, in_specs=placed, out_specs=placed, check_vma=False)
```

time: 604 us -> 138 us (0.23)
  waiting for transfers between devices: 432 us -> 0 us
  Pallas kernels: 0 us -> 132 us
  blocking collectives: 50.9 us -> 0 us
  starting transfers between devices: 44.8 us -> 0 us
  other arithmetic: 31.4 us -> 0 us
  matrix products: 24.9 us -> 0 us
  between operations: 14 us -> 0.65 us
    psum x2 -> x0, waiting for transfers between devices: 228 us -> none  [the longest x1 124 us: body(): trace_gram = lax.psum(contract_last(new_full, new_full), 'tm')]
    reduce_scatter x2 -> x0, waiting for transfers between devices: 151 us -> none  [the longest x1 78.4 us: body(): lax.psum_scatter(matmul_hi(part, pixels), 'pix', scatter_dimension=0, til...]
    pallas_call x0 -> x1, Pallas kernels: none -> 132 us  [body(): pl.pallas_call(kernel, out_shape=(jax.ShapeDtypeStruct(raw_movie.shape, F...]
    all_gather x2 -> x0, blocking collectives: 50.9 us -> none  [the longest x1 26.6 us: body(): trace_full = lax.all_gather(traces, 'pix', axis=0, tiled=True)]
    ppermute x8 -> x0, starting transfers between devices: 44.4 us -> none  [the longest x4 39.2 us: with_halo(): lax.ppermute(tail, axis, [(i, (i + 1) % count) for i in range(ends)])]
    all_gather x1 -> x0, waiting for transfers between devices: 41 us -> none  [body(): foot_full = lax.all_gather(footprints, 'tm', axis=0, tiled=True)]
    add x4 -> x0, other arithmetic: 29.8 us -> none  [substep(): return middle + step_size * summed]
    dot_general x6 -> x0, matrix products: 24.9 us -> none  [the longest x3 13.4 us: contract_last(): lax.dot_general(left, right, (((1,), (1,)), ((), ())), precision=lax.Prec...]
  transfers between devices with their start and end apart: 13 -> 0, of which waited for: 13 -> 0; matrix products, arithmetic and copies ran while one was open for 6% -> 0% of each run, Pallas kernels for 0% -> 0%
where the time goes in v1:
time: 138 us
  Pallas kernels  132 us (96%)
  local copies, waits for them, and re-layouts  4.94 us (4%)
    pallas_call x1, Pallas kernels, body(): pl.pallas_call(kernel, out_shape=(jax.ShapeDtypeStruct(raw_movie.shape, F...  132 us
    unnamed x7, local copies, waits for them, and re-layouts  4.94 us

profile of v1, /device:TPU:2, one launch (start us, length us, event | category | flops | bytes accessed | tf_op | source)
XLA Modules:
  0.0 138.1 jit_solution(10293965011786734215)
XLA Ops:
  0.6 0.0 copy-start
  0.6 0.9 copy-done
  1.5 0.0 copy-start.1
  1.5 0.8 copy-done.1
  2.3 132.5 %shard_map.58 = (f32[8,256,512]{2,1,0:T(8,128)S(1)}, f32[16,2048]{1,0:T(8,128)S(1)}, f32[16,512]{1,0:T(8,128)S(1)}) custom-call(f32[8,256,512]{2,1,0:T(8,128)} %raw.1, f32[16,2048]{1,0:T(8,128)S(1)} %copy-done, f32[16,512]{1,0:T(8,128)S(1)} %copy-done.1), custom_call_target="tpu_custom_call" | custom-call | flops 4000000000 | bytes 16777216 | tf_op jit(solution)/shard_map/pallas_call | solution.py:427
  134.8 2.0 %copy.9 = f32[8,256,512]{2,1,0:T(8,128)} copy(f32[8,256,512]{2,1,0:T(8,128)S(1)} %get-tuple-element.6) | data formatting | bytes 8388608
  136.8 0.7 copy.10
  137.4 0.6 copy.11
Async XLA Ops:
  0.6 0.9 copy-start
  1.5 0.8 copy-start.1

commit v2 on v1

--- a/solution.py
+++ b/solution.py
@@ -47,7 +47,7 @@
 def kernel(
     raw, foot, traces, den_out, foot_out, trace_out,
     y_buf, fd_buf, ph, plo, ff, fh8, fl8, fn, lu, ld, lx, gp, gcr, gl, tf, scale_buf,
-    np_buf, cr_buf, lc_buf, nf,
+    np_buf, cr_buf, lc_buf, nf, pth, ptl,
     loc_sem, out_sem, halo_s, halo_r, fx_s, fx_r, fr_s, fr_r, ring_s, ring_r, rx_s, rx_r,
     core_s, core_r, chip_s, chip_r,
 ):
@@ -173,49 +173,84 @@
             cps.append(send(src, dst, chip_s.at[slot, i], chip_r.at[slot, i], peer_chip(i)))
         return cps
 
-    def diffuse(c):
-        def substep(s, carry):
-            src = jnp.where(lax.rem(s, 2) == 1, c, CHUNKS)
-            dst = jnp.where(lax.rem(s, 2) == 1, CHUNKS, c)
-            col = lax.broadcasted_iota(jnp.int32, (COLS, CHUNK), 0)
-            first = s - 1
-            c0 = y_buf[src, first + 1] - y_buf[src, first]
-            fd_buf[...] = c0 / flux_den(c0)
-
-            def row(r, carry):
-                u = y_buf[src, r]
-                cd = y_buf[src, r + 1] - u
-                ur = jnp.where(col == COLS - 1, 0.0, pltpu.roll(u, COLS - 1, 0))
-                cr = ur - u
-                dd = flux_den(cd)
-                dr = flux_den(cr)
-                inv = 1.0 / (dd * dr)
-                fdn = cd * (dr * inv)
-                frt = cr * (dd * inv)
-                u0 = u[0:8]
-                edge = u0 / flux_den(u0)
-                edge = jnp.concatenate([edge, frt[8:]], axis=0)
-                fl = jnp.where(col == 0, edge, pltpu.roll(frt, 1, 0))
-                total = (fdn - fd_buf[...]) + (frt - fl)
-                fd_buf[...] = fdn
-                new = u + STEP * total
-                outside = ((p == 0) & (r < HALO)) | ((p == NPIX - 1) & (r >= HALO + ROWS))
-                y_buf[dst, r] = jnp.where(outside, 0.0, new)
-                return carry
-
-            return lax.fori_loop(s, EXT - s, row, carry)
-
-        lax.fori_loop(1, HALO + 1, substep, 0)
-        for r in range(ROWS):
+    def rows(c, s, lo, hi):
+        src = jnp.where(lax.rem(s, 2) == 1, c, CHUNKS)
+        dst = jnp.where(lax.rem(s, 2) == 1, CHUNKS, c)
+        col = lax.broadcasted_iota(jnp.int32, (COLS, CHUNK), 0)
+        c0 = y_buf[src, lo] - y_buf[src, lo - 1]
+        fd_buf[...] = c0 / flux_den(c0)
+
+        def row(r, carry):
+            u = y_buf[src, r]
+            cd = y_buf[src, r + 1] - u
+            ur = jnp.where(col == COLS - 1, 0.0, pltpu.roll(u, COLS - 1, 0))
+            cr = ur - u
+            dd = flux_den(cd)
+            dr = flux_den(cr)
+            inv = 1.0 / (dd * dr)
+            fdn = cd * (dr * inv)
+            frt = cr * (dd * inv)
+            u0 = u[0:8]
+            edge = u0 / flux_den(u0)
+            edge = jnp.concatenate([edge, frt[8:]], axis=0)
+            fl = jnp.where(col == 0, edge, pltpu.roll(frt, 1, 0))
+            total = (fdn - fd_buf[...]) + (frt - fl)
+            fd_buf[...] = fdn
+            new = u + STEP * total
+            outside = ((p == 0) & (r < HALO)) | ((p == NPIX - 1) & (r >= HALO + ROWS))
+            y_buf[dst, r] = jnp.where(outside, 0.0, new)
+            return carry
+
+        lax.fori_loop(lo, hi, row, 0)
+
+    def halves(c):
+        def body(r, carry):
             hi, lo = split(y_buf[c, HALO + r])
             ph[c, r] = hi
             plo[c, r] = lo
+            return carry
+
+        lax.fori_loop(0, ROWS, body, 0)
+
+    def diffuse(c):
+        def substep(s, carry):
+            rows(c, s, s, EXT - s)
+            return carry
+
+        lax.fori_loop(1, HALO + 1, substep, 0)
+        halves(c)
+
+    def diffuse_inner(c):
+        def substep(s, carry):
+            rows(c, s, HALO + s, HALO + ROWS - s)
+            return carry
+
+        lax.fori_loop(1, HALO, substep, 0)
+
+    def diffuse_outer(c):
+        def substep(k, carry):
+            s = 1 + k // 2
+            lo = jnp.where(lax.rem(k, 2) == 0, s, EXT - HALO - s)
+            rows(c, s, lo, lo + HALO)
+            return carry
+
+        lax.fori_loop(0, 2 * HALO, substep, 0)
+        halves(c)
+
+    def flip(c):
+        def body(r, carry):
+            hi, lo = split(y_buf[c, HALO + r].T)
+            pth[r, c * CHUNK : (c + 1) * CHUNK] = hi
+            ptl[r, c * CHUNK : (c + 1) * CHUNK] = lo
+            return carry
+
+        lax.fori_loop(0, ROWS, body, 0)
 
     def numerator(c):
         def body(r, acc):
             return acc + dot3(fh8[r], fl8[r], ph[c, r], plo[c, r], 0)
 
-        part = lax.fori_loop(0, ROWS, body, jnp.zeros((RANK, CHUNK), F32))
+        part = lax.fori_loop(0, ROWS, body, jnp.zeros((RANK, CHUNK), F32), unroll=True)
         np_buf[c] = part.reshape(CHIPS, 2, BLK, CHUNK)
 
     def rs_core(c):
@@ -241,18 +276,19 @@
             num = num + lc_buf[c, i]
         new = num * scale_buf[:, c * CHUNK : (c + 1) * CHUNK]
         trace_out[:, c * CHUNK : (c + 1) * CHUNK] = new
-        nf[c, chip, core] = new
-        return gather_chips(nf.at[c, chip, core], nf.at[c, chip, core], CHUNKS + c)
+        mine = nf.at[chip, core, :, pl.ds(c * CHUNK, CHUNK)]
+        mine[...] = new
+        return gather_chips(mine, mine, CHUNKS + c)
 
     def ag_core(c, cps):
         wait_all(cps)
-        return send(
-            nf.at[c, :, core], nf.at[c, :, core], core_s.at[CHUNKS + c], core_r.at[CHUNKS + c], sibling
-        )
-
-    def foot_update(c, cp):
-        cp.wait_recv()
-        nh, nl = split(nf[c].reshape(RANK, CHUNK))
+        mine = nf.at[:, core, :, pl.ds(c * CHUNK, CHUNK)]
+        return send(mine, mine, core_s.at[CHUNKS + c], core_r.at[CHUNKS + c], sibling)
+
+    def foot_update(c, n, cps):
+        wait_all(cps)
+        lo, hi = c * CHUNK, (c + n) * CHUNK
+        nh, nl = split(nf[:, :, :, lo:hi].reshape(RANK, n * CHUNK))
         first = c == 0
 
         def put(where, val):
@@ -262,33 +298,33 @@
         put(pl.ds(LOCAL, RANK), dot3(nh, nl, nh, nl, 1))
 
         def body(r, carry):
-            put(pl.ds(pl.multiple_of(r * COLS, COLS), COLS), dot3(nh, nl, ph[c, r], plo[c, r], 1))
-            return carry
-
-        lax.fori_loop(0, ROWS, body, 0)
-
-    halo_start(0)
+            put(
+                pl.ds(pl.multiple_of(r * COLS, COLS), COLS),
+                dot3(nh, nl, pth[r, lo:hi], ptl[r, lo:hi], 0),
+            )
+            return carry
+
+        lax.fori_loop(0, ROWS, body, 0, unroll=True)
+
     fx = send(foot, ff.at[t], fx_s.at[0], fx_r.at[0], across)
     own0 = foot_send(0, 1)
-    tr = gather_chips(traces, tf.at[chip, core], 2 * CHUNKS)
+    halo_start(0)
     halo_start(1)
+    halo_start(2)
+    halo_start(3)
     fx.wait_recv()
     oth0 = foot_send(0, 0)
     wait_all(own0)
     own1 = foot_send(1, 1)
     wait_all(oth0)
     oth1 = foot_send(1, 0)
-    wait_all(tr)
-    trace_load.wait()
-    tr_core = send(tf.at[:, core], tf.at[:, core], core_s.at[2 * CHUNKS], core_r.at[2 * CHUNKS], sibling)
+    for cp in loads:
+        cp.wait()
+    halo_wait(0)
     wait_all(own1)
     own2 = foot_send(2, 1)
     wait_all(oth1)
     oth2 = foot_send(2, 0)
-    for cp in loads:
-        cp.wait()
-    halo_wait(0)
-    halo_start(2)
     diffuse(0)
     stores = []
 
@@ -305,8 +341,8 @@
     wait_all(oth2)
     oth3 = foot_send(3, 0)
     foot_load.wait()
+    trace_load.wait()
     halo_wait(1)
-    halo_start(3)
     diffuse(1)
     store(1)
     wait_all(own3)
@@ -323,11 +359,25 @@
     def gram_body(r, acc):
         return acc + dot3(fh8[r], fl8[r], fh8[r], fl8[r], 1)
 
-    gp[...] = lax.fori_loop(0, ROWS, gram_body, jnp.zeros((RANK, RANK), F32)).reshape(CHIPS, 2, BLK, RANK)
+    gp[...] = lax.fori_loop(0, ROWS, gram_body, jnp.zeros((RANK, RANK), F32), unroll=True).reshape(CHIPS, 2, BLK, RANK)
     gslot = 2 * CHUNKS + 1
     g_core = send(gp.at[:, 1 - core], gcr, core_s.at[gslot], core_r.at[gslot], sibling)
     numerator(0)
     rs0 = rs_core(0)
+    numerator(1)
+    rs1 = rs_core(1)
+    halo_wait(2)
+    diffuse(2)
+    store(2)
+    numerator(2)
+    rs2 = rs_core(2)
+    diffuse_inner(3)
+    flip(0)
+    flip(1)
+    flip(2)
+    halo_wait(3)
+
+    tr = gather_chips(traces, tf.at[chip, core], 2 * CHUNKS)
     g_core.wait_recv()
     gcr[...] = gcr[...] + gp[:, core]
     g_chips = []
@@ -336,41 +386,35 @@
             send(gcr.at[lax.rem(chip + i, CHIPS)], gl.at[i], chip_s.at[gslot, i], chip_r.at[gslot, i], peer_chip(i))
         )
     rs0 = rs_chips(0, rs0)
-    numerator(1)
-    rs1 = rs_core(1)
     rs1 = rs_chips(1, rs1)
+    rs2 = rs_chips(2, rs2)
+    diffuse_outer(3)
+    store(3)
+    numerator(3)
+    rs3 = rs_core(3)
+    wait_all(tr)
+    tr_core = send(tf.at[:, core], tf.at[:, core], core_s.at[2 * CHUNKS], core_r.at[2 * CHUNKS], sibling)
     wait_all(g_chips)
     gram = gcr[chip]
     for i in range(1, CHIPS):
         gram = gram + gl[i]
+    rs3 = rs_chips(3, rs3)
+    flip(3)
     tr_core.wait_recv()
     gh, gl_ = split(gram)
     th, tl = split(tf[...].reshape(RANK, FRAMES))
     scale_buf[...] = tf[chip, core] / dot3(gh, gl_, th, tl, 0)
     ag0 = ag_chips(0, rs0)
-    halo_wait(2)
-    diffuse(2)
-    store(2)
+    ag1 = ag_chips(1, rs1)
+    ag2 = ag_chips(2, rs2)
+    ag3 = ag_chips(3, rs3)
     ag0 = ag_core(0, ag0)
-    ag1 = ag_chips(1, rs1)
-    numerator(2)
-    rs2 = rs_core(2)
-    foot_update(0, ag0)
-    rs2 = rs_chips(2, rs2)
     ag1 = ag_core(1, ag1)
-    foot_update(1, ag1)
-    halo_wait(3)
-    diffuse(3)
-    store(3)
-    ag2 = ag_chips(2, rs2)
-    numerator(3)
-    rs3 = rs_core(3)
-    rs3 = rs_chips(3, rs3)
     ag2 = ag_core(2, ag2)
-    foot_update(2, ag2)
-    ag3 = ag_chips(3, rs3)
+    foot_update(0, 2, (ag0, ag1))
+    foot_update(2, 1, (ag2,))
     ag3 = ag_core(3, ag3)
-    foot_update(3, ag3)
+    foot_update(3, 1, (ag3,))
 
     def ring_send(s, j, got):
         cps = []
@@ -409,7 +453,7 @@
         foot_out[:, w] = ff[t, :, w] * (lu[3, 1, :, w] + lx[:, w]) / den
         return carry
 
-    lax.fori_loop(0, ROWS, final, 0)
+    lax.fori_loop(0, ROWS, final, 0, unroll=True)
 
     for cp in pending:
         cp.wait_send()
@@ -453,7 +497,9 @@
             vm((CHUNKS, CHIPS, 2, BLK, CHUNK), F32),
             vm((CHUNKS, CHIPS, BLK, CHUNK), F32),
             vm((CHUNKS, CHIPS, BLK, CHUNK), F32),
-            vm((CHUNKS, CHIPS, 2, BLK, CHUNK), F32),
+            vm((CHIPS, 2, BLK, FRAMES), F32),
+            vm((ROWS, FRAMES, COLS), BF16),
+            vm((ROWS, FRAMES, COLS), BF16),
             dma((CHUNKS + 2,)),
             dma((CHUNKS,)),
             dma((2, CHUNKS)),

time: 138 us -> 115 us (0.83)
  Pallas kernels: 132 us -> 109 us
    pallas_call x1, Pallas kernels: 132 us -> 109 us  [body(): pl.pallas_call(kernel, out_shape=(jax.ShapeDtypeStruct(raw_movie.shape, F...]
where the time goes in v2:
time: 115 us
  Pallas kernels  109 us (95%)
  local copies, waits for them, and re-layouts  4.94 us (4%)
    pallas_call x1, Pallas kernels, body(): pl.pallas_call(kernel, out_shape=(jax.ShapeDtypeStruct(raw_movie.shape, F...  109 us
    unnamed x7, local copies, waits for them, and re-layouts  4.94 us

profile of v2, /device:TPU:2, one launch (start us, length us, event | category | flops | bytes accessed | tf_op | source)
XLA Modules:
  0.0 114.9 jit_solution(16851866385576673881)
XLA Ops:
  0.6 0.0 copy-start
  0.6 0.9 copy-done
  1.5 0.0 copy-start.1
  1.5 0.8 copy-done.1
  2.3 109.3 %shard_map.58 = (f32[8,256,512]{2,1,0:T(8,128)S(1)}, f32[16,2048]{1,0:T(8,128)S(1)}, f32[16,512]{1,0:T(8,128)S(1)}) custom-call(f32[8,256,512]{2,1,0:T(8,128)} %raw.1, f32[16,2048]{1,0:T(8,128)S(1)} %copy-done, f32[16,512]{1,0:T(8,128)S(1)} %copy-done.1), custom_call_target="tpu_custom_call" | custom-call | flops 4000000000 | bytes 16777216 | tf_op jit(solution)/shard_map/pallas_call | solution.py:471
  111.6 2.0 %copy.9 = f32[8,256,512]{2,1,0:T(8,128)} copy(f32[8,256,512]{2,1,0:T(8,128)S(1)} %get-tuple-element.6) | data formatting | bytes 8388608
  113.6 0.7 copy.10
  114.3 0.6 copy.11
Async XLA Ops:
  0.6 0.9 copy-start
  1.5 0.8 copy-start.1

commit v3 on v2

--- a/solution.py
+++ b/solution.py
@@ -24,6 +24,8 @@
 LOCAL = ROWS * COLS
 WIDE = LOCAL + RANK
 STEP = 0.24
+PART = 1024
+REST = WIDE - PART
 
 
 def split(x):
@@ -47,9 +49,9 @@
 def kernel(
     raw, foot, traces, den_out, foot_out, trace_out,
     y_buf, fd_buf, ph, plo, ff, fh8, fl8, fn, lu, ld, lx, gp, gcr, gl, tf, scale_buf,
-    np_buf, cr_buf, lc_buf, nf, pth, ptl,
+    np_buf, cr_buf, lc_buf, nf, pth, ptl, xb, lub, ldb,
     loc_sem, out_sem, halo_s, halo_r, fx_s, fx_r, fr_s, fr_r, ring_s, ring_r, rx_s, rx_r,
-    core_s, core_r, chip_s, chip_r,
+    core_s, core_r, chip_s, chip_r, rest_s, rest_r,
 ):
     p = lax.axis_index("pix")
     t = lax.axis_index("tm")
@@ -416,6 +418,9 @@
     ag3 = ag_core(3, ag3)
     foot_update(3, 1, (ag3,))
 
+    def low(ref, b):
+        return ref.at[b, :, pl.ds(0, PART)]
+
     def ring_send(s, j, got):
         cps = []
         for d in range(2):
@@ -424,36 +429,78 @@
             land = lu if d == 0 else ld
             b = fblock(j, (NZ // 2 - s) * (1 if d == 0 else -1))
             if d in got:
-                land[s - 1, j] = land[s - 1, j] + fn[b]
+                land[s - 1, j] = land[s - 1, j] + fn[b, :, :PART]
                 src = land.at[s - 1, j]
             else:
-                src = fn.at[b]
+                src = low(fn, b)
             cps.append(send(src, land.at[s, j], ring_s.at[d, s, j], ring_r.at[d, s, j], up if d == 0 else down))
         return cps
 
+    cross = {}
+    for dz in (4, 3, -3, 2, -2, 1, -1, 0):
+        k = dz % NZ
+        cross[dz] = send(
+            fn.at[fblock(0, dz), :, pl.ds(PART, REST)], xb.at[k], rx_s.at[k], rx_r.at[k], across
+        )
+
+    def take(dz):
+        cross[dz].wait_recv()
+        k = dz % NZ
+        xb[k] = xb[k] + fn[fblock(1, dz), :, PART:]
+
+    def rest_send(s, cps):
+        if s == 0:
+            take(4)
+        else:
+            take(4 - s)
+            take(s - 4)
+            wait_all(cps)
+        out = []
+        for d in range(2):
+            land = lub if d == 0 else ldb
+            k = ((4 - s) * (1 if d == 0 else -1)) % NZ
+            w = pl.ds(d * (REST // 2), REST // 2) if s <= 1 else pl.ds(0, REST)
+            if s > 0:
+                xb[k, :, w] = xb[k, :, w] + land[s - 1, :, w]
+            w = w if s == 0 else pl.ds(0, REST)
+            out.append(
+                send(xb.at[k, :, w], land.at[s, :, w], rest_s.at[d, s], rest_r.at[d, s], up if d == 0 else down)
+            )
+        return out
+
     r0 = ring_send(0, 0, ())
     r1 = ring_send(0, 1, ())
+    rb = rest_send(0, ())
     for s in range(1, 4):
         wait_all(r0)
         r0 = ring_send(s, 0, (1,) if s == 1 else (0, 1))
         wait_all(r1)
         r1 = ring_send(s, 1, (0,) if s == 1 else (0, 1))
+        rb = rest_send(s, rb)
     wait_all(r0)
-    bo = fblock(0, 0)
-    lu[3, 0] = (lu[3, 0] + ld[3, 0]) + fn[bo]
-    rx = send(lu.at[3, 0], lx, rx_s.at[0], rx_r.at[0], across)
+    lu[3, 0] = (lu[3, 0] + ld[3, 0]) + fn[fblock(0, 0), :, :PART]
+    rx = send(lu.at[3, 0], lx, rx_s.at[NZ], rx_r.at[NZ], across)
     wait_all(r1)
-    lu[3, 1] = (lu[3, 1] + ld[3, 1]) + fn[fblock(1, 0)]
+    lu[3, 1] = (lu[3, 1] + ld[3, 1]) + fn[fblock(1, 0), :, :PART]
+    take(0)
+    wait_all(rb)
+    xb[0] = xb[0] + (lub[3] + ldb[3])
+    kh, kl = split(xb[0, :, LOCAL - PART :])
+
+    def final(r):
+        w = slice(r * COLS, (r + 1) * COLS)
+        den = dot3(kh, kl, fh8[r], fl8[r], 0)
+        if w.start >= PART:
+            num = xb[0, :, w.start - PART : w.stop - PART]
+        else:
+            num = lu[3, 1, :, w] + lx[:, w]
+        foot_out[:, w] = ff[t, :, w] * num / den
+
+    for r in range(PART // COLS, ROWS):
+        final(r)
     rx.wait_recv()
-    kh, kl = split(lu[3, 1, :, pl.ds(LOCAL, RANK)] + lx[:, pl.ds(LOCAL, RANK)])
-
-    def final(r, carry):
-        w = pl.ds(pl.multiple_of(r * COLS, COLS), COLS)
-        den = dot3(kh, kl, fh8[r], fl8[r], 0)
-        foot_out[:, w] = ff[t, :, w] * (lu[3, 1, :, w] + lx[:, w]) / den
-        return carry
-
-    lax.fori_loop(0, ROWS, final, 0, unroll=True)
+    for r in range(PART // COLS):
+        final(r)
 
     for cp in pending:
         cp.wait_send()
@@ -463,12 +510,26 @@
         cp.wait()
 
 
+def move_out(den, foot, trace, den_hbm, foot_hbm, trace_hbm, sems):
+    cps = [pltpu.make_async_copy(den.at[r], den_hbm.at[r], sems.at[r]) for r in range(ROWS)]
+    cps.append(pltpu.make_async_copy(foot, foot_hbm, sems.at[ROWS]))
+    cps.append(pltpu.make_async_copy(trace, trace_hbm, sems.at[ROWS + 1]))
+    for cp in cps:
+        cp.start()
+    for cp in cps:
+        cp.wait()
+
+
+def stay(x):
+    return pltpu.with_memory_space_constraint(x, pltpu.MemorySpace.HBM)
+
+
 def body(raw_movie, footprints, traces):
     dma = pltpu.SemaphoreType.DMA
     vm = pltpu.VMEM
     hbm = pl.BlockSpec(memory_space=pltpu.MemorySpace.HBM)
     inv = pl.BlockSpec(memory_space=pltpu.MemorySpace.VMEM)
-    return pl.pallas_call(
+    outs = pl.pallas_call(
         kernel,
         out_shape=(
             jax.ShapeDtypeStruct(raw_movie.shape, F32),
@@ -476,7 +537,7 @@
             jax.ShapeDtypeStruct(traces.shape, F32),
         ),
         in_specs=[hbm, hbm, hbm],
-        out_specs=(hbm, inv, inv),
+        out_specs=(inv, inv, inv),
         scratch_shapes=[
             vm((CHUNKS + 1, EXT, COLS, CHUNK), F32),
             vm((COLS, CHUNK), F32),
@@ -486,9 +547,9 @@
             vm((ROWS, RANK, COLS), BF16),
             vm((ROWS, RANK, COLS), BF16),
             vm((NB, BLK, WIDE), F32),
-            vm((4, 2, BLK, WIDE), F32),
-            vm((4, 2, BLK, WIDE), F32),
-            vm((BLK, WIDE), F32),
+            vm((4, 2, BLK, PART), F32),
+            vm((4, 2, BLK, PART), F32),
+            vm((BLK, PART), F32),
             vm((CHIPS, 2, BLK, RANK), F32),
             vm((CHIPS, BLK, RANK), F32),
             vm((CHIPS, BLK, RANK), F32),
@@ -500,6 +561,9 @@
             vm((CHIPS, 2, BLK, FRAMES), F32),
             vm((ROWS, FRAMES, COLS), BF16),
             vm((ROWS, FRAMES, COLS), BF16),
+            vm((NZ, BLK, REST), F32),
+            vm((4, BLK, REST), F32),
+            vm((4, BLK, REST), F32),
             dma((CHUNKS + 2,)),
             dma((CHUNKS,)),
             dma((2, CHUNKS)),
@@ -510,18 +574,28 @@
             dma((2, 4, 2)),
             dma((2, 4, 2)),
             dma((2, 4, 2)),
-            dma((1,)),
-            dma((1,)),
+            dma((NZ + 1,)),
+            dma((NZ + 1,)),
             dma((2 * CHUNKS + 2,)),
             dma((2 * CHUNKS + 2,)),
             dma((2 * CHUNKS + 2, CHIPS)),
             dma((2 * CHUNKS + 2, CHIPS)),
+            dma((2, 4)),
+            dma((2, 4)),
         ],
         compiler_params=pltpu.CompilerParams(
             collective_id=0, has_side_effects=True, vmem_limit_bytes=48 * 1024 * 1024
         ),
         cost_estimate=pl.CostEstimate(flops=4 * 10**9, bytes_accessed=16 * 2**20, transcendentals=0),
-    )(raw_movie, footprints, traces)
+    )(raw_movie, stay(footprints), stay(traces))
+    return pl.pallas_call(
+        move_out,
+        out_shape=tuple(jax.ShapeDtypeStruct(o.shape, F32) for o in outs),
+        in_specs=[inv, inv, inv],
+        out_specs=(hbm, hbm, hbm),
+        scratch_shapes=[dma((ROWS + 2,))],
+        compiler_params=pltpu.CompilerParams(vmem_limit_bytes=8 * 1024 * 1024),
+    )(*outs)
 
 
 def solution(mesh):

time: 115 us -> 107 us (0.930)
  local copies, waits for them, and re-layouts: 4.94 us -> 0 us
  Pallas kernels: 109 us -> 106 us
    pallas_call x1, Pallas kernels: 109 us -> 104 us  [body(): pl.pallas_call(kernel, out_shape=(jax.ShapeDtypeStruct(raw_movie.shape, F...]
    unnamed x7 -> x0, local copies, waits for them, and re-layouts: 4.94 us -> none
    pallas_call x0 -> x1, Pallas kernels: none -> 2.13 us  [body(): pl.pallas_call(move_out, out_shape=tuple((jax.ShapeDtypeStruct(o.shape, F...]
where the time goes in v3:
time: 107 us
  Pallas kernels  106 us (99%)
    pallas_call x1, Pallas kernels, body(): pl.pallas_call(kernel, out_shape=(jax.ShapeDtypeStruct(raw_movie.shape, F...  104 us

profile of v3, /device:TPU:2, one launch (start us, length us, event | category | flops | bytes accessed | tf_op | source)
XLA Modules:
  0.0 107.0 jit_solution(16084508400355304668)
XLA Ops:
  0.6 104.2 %shard_map.58 = (f32[8,256,512]{2,1,0:T(8,128)S(1)}, f32[16,2048]{1,0:T(8,128)S(1)}, f32[16,512]{1,0:T(8,128)S(1)}) custom-call(f32[8,256,512]{2,1,0:T(8,128)} %raw.1, f32[16,2048]{1,0:T(8,128)} %foot.1, f32[16,512]{1,0:T(8,128)} %traces.1), custom_call_target="tpu_custom_call" | custom-call | flops 4000000000 | bytes 16777216 | tf_op jit(solution)/shard_map/pallas_call | solution.py:532
  104.9 2.1 %shard_map.59 = (f32[8,256,512]{2,1,0:T(8,128)}, f32[16,2048]{1,0:T(8,128)}, f32[16,512]{1,0:T(8,128)}) custom-call(f32[8,256,512]{2,1,0:T(8,128)S(1)} %get-tuple-element.6.den, f32[16,2048]{1,0:T(8,128)S(1)} %get-tuple-element.7.foot, f32[16,512]{1,0:T(8,128)S(1)} %get-tuple-element.8.trace), custom_call_target="tpu_custom_call" | custom-call | tf_op jit(solution)/shard_map/pallas_call | solution.py:591

commit v4 on v3

--- a/solution.py
+++ b/solution.py
@@ -178,14 +178,15 @@
     def rows(c, s, lo, hi):
         src = jnp.where(lax.rem(s, 2) == 1, c, CHUNKS)
         dst = jnp.where(lax.rem(s, 2) == 1, CHUNKS, c)
-        col = lax.broadcasted_iota(jnp.int32, (COLS, CHUNK), 0)
+        sub = lax.broadcasted_iota(jnp.int32, (8, CHUNK), 0)
         c0 = y_buf[src, lo] - y_buf[src, lo - 1]
         fd_buf[...] = c0 / flux_den(c0)
 
         def row(r, carry):
             u = y_buf[src, r]
             cd = y_buf[src, r + 1] - u
-            ur = jnp.where(col == COLS - 1, 0.0, pltpu.roll(u, COLS - 1, 0))
+            ur = pltpu.roll(u, COLS - 1, 0)
+            ur = jnp.concatenate([ur[:-8], jnp.where(sub == 7, 0.0, ur[-8:])], axis=0)
             cr = ur - u
             dd = flux_den(cd)
             dr = flux_den(cr)
@@ -194,8 +195,8 @@
             frt = cr * (dd * inv)
             u0 = u[0:8]
             edge = u0 / flux_den(u0)
-            edge = jnp.concatenate([edge, frt[8:]], axis=0)
-            fl = jnp.where(col == 0, edge, pltpu.roll(frt, 1, 0))
+            fl = pltpu.roll(frt, 1, 0)
+            fl = jnp.concatenate([jnp.where(sub == 0, edge, fl[:8]), fl[8:]], axis=0)
             total = (fdn - fd_buf[...]) + (frt - fl)
             fd_buf[...] = fdn
             new = u + STEP * total
@@ -436,6 +437,8 @@
             cps.append(send(src, land.at[s, j], ring_s.at[d, s, j], ring_r.at[d, s, j], up if d == 0 else down))
         return cps
 
+    sent = list(pending)
+    pending.clear()
     cross = {}
     for dz in (4, 3, -3, 2, -2, 1, -1, 0):
         k = dz % NZ
@@ -470,6 +473,12 @@
 
     r0 = ring_send(0, 0, ())
     r1 = ring_send(0, 1, ())
+    for cp in sent:
+        cp.wait_send()
+    for c in range(CHUNKS):
+        halo_wait_send(c)
+    for cp in stores:
+        cp.wait()
     rb = rest_send(0, ())
     for s in range(1, 4):
         wait_all(r0)
@@ -504,10 +513,6 @@
 
     for cp in pending:
         cp.wait_send()
-    for c in range(CHUNKS):
-        halo_wait_send(c)
-    for cp in stores:
-        cp.wait()
 
 
 def move_out(den, foot, trace, den_hbm, foot_hbm, trace_hbm, sems):

time: 107 us -> 107 us (level)
  no operation moved by 1% of the time
where the time goes in v4:
time: 107 us
  Pallas kernels  106 us (99%)
    pallas_call x1, Pallas kernels, body(): pl.pallas_call(kernel, out_shape=(jax.ShapeDtypeStruct(raw_movie.shape, F...  104 us

profile of v4, /device:TPU:2, one launch (start us, length us, event | category | flops | bytes accessed | tf_op | source)
XLA Modules:
  0.0 106.8 jit_solution(2692258092071340187)
XLA Ops:
  0.6 104.1 %shard_map.58 = (f32[8,256,512]{2,1,0:T(8,128)S(1)}, f32[16,2048]{1,0:T(8,128)S(1)}, f32[16,512]{1,0:T(8,128)S(1)}) custom-call(f32[8,256,512]{2,1,0:T(8,128)} %raw.1, f32[16,2048]{1,0:T(8,128)} %foot.1, f32[16,512]{1,0:T(8,128)} %traces.1), custom_call_target="tpu_custom_call" | custom-call | flops 4000000000 | bytes 16777216 | tf_op jit(solution)/shard_map/pallas_call | solution.py:537
  104.7 2.1 %shard_map.59 = (f32[8,256,512]{2,1,0:T(8,128)}, f32[16,2048]{1,0:T(8,128)}, f32[16,512]{1,0:T(8,128)}) custom-call(f32[8,256,512]{2,1,0:T(8,128)S(1)} %get-tuple-element.6.den, f32[16,2048]{1,0:T(8,128)S(1)} %get-tuple-element.7.foot, f32[16,512]{1,0:T(8,128)S(1)} %get-tuple-element.8.trace), custom_call_target="tpu_custom_call" | custom-call | tf_op jit(solution)/shard_map/pallas_call | solution.py:596
